TPU v7x, 32 devices: a whole 2x2x4 slice. The times are simulated.
32 devices in a mesh: fsdp: 4 (over x, core), tok: 8 (over z, y).
Axes of the slice: x: 2, y: 2, z: 4, core: 2. Of those that a mesh axis runs over, the one named last changes fastest.
Arguments:
- states: bfloat16 [4, 512, 1024], P('fsdp', 'tok'), may hold values from -8 to 8
- cache_keys: bfloat16 [4, 1024, 1024], P('fsdp', 'tok'), may hold values from -6 to 6
- cache_values: bfloat16 [4, 1024, 1024], P('fsdp', 'tok'), may hold values from -6 to 6
- cache_len: int32 [4], P('fsdp'), may hold values from 1 to 1024, as said below
- token_slot: int32 [4, 512], P('fsdp', 'tok'), may hold values from 0 to 511, as said below
- bucket_table: int32 [1536], replicated, may hold values from 0 to 31
- rel_bias: float32 [32, 16], replicated, may hold values from -3 to 250
- norm_gain: float32 [1024], replicated, may hold values from 0.5 to 1.5
- w_query: bfloat16 [1024, 1024], P(('fsdp', 'tok')), may hold values from -0.0234375 to 0.0234375
- w_key: bfloat16 [1024, 1024], P(('fsdp', 'tok')), may hold values from -0.1875 to 0.1875
- w_value: bfloat16 [1024, 1024], P(('fsdp', 'tok')), may hold values from -0.1875 to 0.1875
- w_out: bfloat16 [1024, 1024], P(('fsdp', 'tok')), may hold values from -1.5 to 1.5
Outputs:
- hidden_out: bfloat16 [4, 512, 1024], P('fsdp', 'tok')
- new_keys: bfloat16 [4, 512, 1024], P('fsdp', 'tok')
- new_values: bfloat16 [4, 512, 1024], P('fsdp', 'tok')
Inputs may be any that keep to these rules, and one draw needn't show every extreme that they name: `cache_len`: one request has exactly 1024 live rows. `token_slot`: each row is a permutation of 0 to 511; every aligned block of 64 tokens of a request has exactly 8 of its slots in each aligned block of 64 slots.
All inputs are finite; a program needn't handle non-finite values.
Results may differ from a plain program's by a relative error of at most 0.0095.
Values may be sent and summed in bfloat16 or wider, within the bound.
No kernel may reach another device: no remote copies, remote signals or barrier semaphores. Data moves between devices by JAX's collectives and lax.ppermute only.
A program may use at most 64 MiB of HBM per device.

v0:
```python
import jax
import jax.numpy as jnp
from jax import lax
from jax.sharding import PartitionSpec as P

far_away = 1073741824
neg_floor = -1e30


def bias_scores(bucket_ids, bias_parts):
    bucket_count = bias_parts[0].shape[0]
    one_hot = (bucket_ids[..., None] == jnp.arange(bucket_count, dtype=jnp.int32)).astype(
        jnp.bfloat16
    )
    high_part = jnp.einsum(
        "qkb,bh->hqk", one_hot, bias_parts[0], preferred_element_type=jnp.float32
    )
    middle = jnp.einsum("qkb,bh->hqk", one_hot, bias_parts[1], preferred_element_type=jnp.float32)
    low_part = jnp.einsum("qkb,bh->hqk", one_hot, bias_parts[2], preferred_element_type=jnp.float32)
    return high_part + middle + low_part


def absorb(running, queries, query_pos, keys_here, values_here, key_pos, bucket_table, bias_parts):
    totals, peak_old, masses = running
    head_count = queries.shape[1]
    keys_split = keys_here.reshape(keys_here.shape[0], head_count, -1)
    values_split = values_here.reshape(values_here.shape[0], head_count, -1)
    scores = jnp.einsum("qhd,khd->hqk", queries, keys_split, preferred_element_type=jnp.float32)
    distance = query_pos[:, None] - key_pos[None, :]
    allowed = (distance >= 0)[None]
    bucket_ids = jnp.take(bucket_table, jnp.clip(distance, 0, bucket_table.shape[0] - 1), axis=0)
    scores = scores + bias_scores(bucket_ids, bias_parts)
    new_peak = jnp.maximum(peak_old, jnp.max(jnp.where(allowed, scores, neg_floor), axis=-1))
    weights = jnp.where(allowed, jnp.exp(scores - new_peak[..., None]), 0.0)
    shrink = jnp.exp(peak_old - new_peak)
    masses = masses * shrink + jnp.sum(weights, axis=-1)
    totals = totals * jnp.transpose(shrink)[..., None] + jnp.einsum(
        "hqk,khd->qhd",
        weights.astype(jnp.bfloat16),
        values_split,
        preferred_element_type=jnp.float32,
    )
    return (totals, new_peak, masses)


def permute_rows(selector, rows):
    return jnp.dot(selector.astype(jnp.bfloat16), rows, preferred_element_type=jnp.float32).astype(
        jnp.bfloat16
    )


def permute_ints(selector, values):
    return jnp.sum(jnp.where(selector, values[None, :], 0), axis=1).astype(jnp.int32)


def shards(
    states,
    cache_keys,
    cache_values,
    cache_len,
    token_slot,
    bucket_table,
    rel_bias,
    norm_gain,
    w_query,
    w_key,
    w_value,
    w_out,
):
    peer_count = lax.axis_size("tok")
    my_index = lax.axis_index("tok")
    tokens = states[0]
    tok_rows = tokens.shape[0]
    feature_count = tokens.shape[1]
    per_peer = tok_rows // peer_count
    head_count = rel_bias.shape[1]
    head_size = feature_count // head_count
    slot_ids = token_slot[0]
    length = cache_len[0]
    row_iota = jnp.arange(tok_rows, dtype=jnp.int32)
    ranking = jnp.sum((slot_ids[None, :] < slot_ids[:, None]).astype(jnp.int32), axis=1)
    sort_sel = ranking[None, :] == row_iota[:, None]
    sent_rows = permute_rows(sort_sel, tokens).reshape(peer_count, per_peer, feature_count)
    sent_slots = permute_ints(sort_sel, slot_ids).reshape(peer_count, per_peer)
    sent_pos = (my_index * tok_rows + permute_ints(sort_sel, row_iota)).reshape(
        peer_count, per_peer
    )
    got_rows, got_slots, got_pos = (
        lax.all_to_all(sent_rows, "tok", split_axis=0, concat_axis=0, tiled=True),
        lax.all_to_all(sent_slots, "tok", split_axis=0, concat_axis=0, tiled=True),
        lax.all_to_all(sent_pos, "tok", split_axis=0, concat_axis=0, tiled=True),
    )
    local_slot = got_slots.reshape(tok_rows) - my_index * tok_rows
    place_sel = local_slot[None, :] == row_iota[:, None]
    dealt = permute_rows(place_sel, got_rows.reshape(tok_rows, feature_count))
    dealt_pos = permute_ints(place_sel, got_pos.reshape(tok_rows))
    query_w, key_w, value_w, out_w = (
        lax.all_gather(w_query, ("fsdp", "tok"), axis=0, tiled=True),
        lax.all_gather(w_key, ("fsdp", "tok"), axis=0, tiled=True),
        lax.all_gather(w_value, ("fsdp", "tok"), axis=0, tiled=True),
        lax.all_gather(w_out, ("fsdp", "tok"), axis=0, tiled=True),
    )
    wide_in = dealt.astype(jnp.float32)
    inverse = lax.rsqrt(jnp.mean(wide_in * wide_in, axis=-1, keepdims=True) + 1e-06)
    normed = (wide_in * inverse * norm_gain).astype(jnp.bfloat16)
    queries = jnp.dot(normed, query_w, preferred_element_type=jnp.float32).astype(jnp.bfloat16)
    new_keys = jnp.dot(normed, key_w, preferred_element_type=jnp.float32).astype(jnp.bfloat16)
    new_values = jnp.dot(normed, value_w, preferred_element_type=jnp.float32).astype(jnp.bfloat16)
    query_pos = length + dealt_pos
    cache_rows = cache_keys.shape[1]
    cache_spot = my_index * cache_rows + jnp.arange(cache_rows, dtype=jnp.int32)
    key_pos = jnp.concatenate([jnp.where(cache_spot < length, cache_spot, far_away), query_pos])
    keys_here = jnp.concatenate([cache_keys[0], new_keys])
    values_here = jnp.concatenate([cache_values[0], new_values])
    bias_high = rel_bias.astype(jnp.bfloat16)
    remainder = rel_bias - bias_high.astype(jnp.float32)
    bias_middle = remainder.astype(jnp.bfloat16)
    bias_low = (remainder - bias_middle.astype(jnp.float32)).astype(jnp.bfloat16)
    bias_parts = (bias_high, bias_middle, bias_low)
    query_heads = queries.reshape(tok_rows, head_count, head_size)
    shard_len = keys_here.shape[0]
    initial = (
        jnp.zeros((tok_rows, head_count, head_size), jnp.float32),
        jnp.full((head_count, tok_rows), neg_floor, jnp.float32),
        jnp.zeros((head_count, tok_rows), jnp.float32),
    )
    running = initial
    part_keys = lax.all_gather(keys_here, "tok", axis=0, tiled=True)
    part_values = lax.all_gather(values_here, "tok", axis=0, tiled=True)
    part_pos = lax.all_gather(key_pos, "tok", axis=0, tiled=True)
    rows_in = part_keys.shape[0]
    block_len = 2 * shard_len
    shard_count = rows_in // block_len
    blocks = (
        part_keys.reshape(shard_count, block_len, feature_count),
        part_values.reshape(shard_count, block_len, feature_count),
        part_pos.reshape(shard_count, block_len),
    )

    def advance(running_in, block_set):
        return (
            absorb(
                running_in,
                query_heads,
                query_pos,
                block_set[0],
                block_set[1],
                block_set[2],
                bucket_table,
                bias_parts,
            ),
            None,
        )

    running, unused = lax.scan(advance, running, blocks)
    totals, peaks, masses = running
    context = (
        (totals / jnp.transpose(masses)[..., None])
        .reshape(tok_rows, feature_count)
        .astype(jnp.bfloat16)
    )
    result_dealt = (wide_in + jnp.dot(context, out_w, preferred_element_type=jnp.float32)).astype(
        jnp.bfloat16
    )
    back_rows = permute_rows(jnp.transpose(place_sel), result_dealt).reshape(
        peer_count, per_peer, feature_count
    )
    returned = lax.all_to_all(back_rows, "tok", split_axis=0, concat_axis=0, tiled=True)
    hidden = permute_rows(jnp.transpose(sort_sel), returned.reshape(tok_rows, feature_count))
    return (hidden[None], new_keys[None], new_values[None])


def solution(mesh):
    in_specs = (
        P("fsdp", "tok", None),
        P("fsdp", "tok", None),
        P("fsdp", "tok", None),
        P("fsdp"),
        P("fsdp", "tok"),
        P(),
        P(),
        P(),
        P(("fsdp", "tok"), None),
        P(("fsdp", "tok"), None),
        P(("fsdp", "tok"), None),
        P(("fsdp", "tok"), None),
    )
    out_specs = (P("fsdp", "tok", None), P("fsdp", "tok", None), P("fsdp", "tok", None))
    return jax.shard_map(shards, mesh=mesh, in_specs=in_specs, out_specs=out_specs, check_vma=False)
```

profile of v0, /device:TPU:0, one launch (start us, length us, event | category | flops | bytes accessed | tf_op | source)
XLA Modules:
  0.0 936.9 jit_solution(472488924100509051)
XLA Ops:
  11.8 7.3 all-to-all-start
  19.9 5.6 all-to-all-done
  25.4 3.4 all-to-all-start.1
  29.0 7.2 all-to-all-done.1
  38.0 32.8 %all-gather.13.cloned.1.call-done = bf16[1024,1024]{1,0:T(8,128)(2,1)} async-done(((bf16[32,1024]{1,0:T(8,128)(2,1)}), bf16[1024,1024]{1,0:T(8,128)(2,1)}) %all-gather.13.cloned.1.call-update) | async-done | bytes 2097168 | tf_op jit(solution)/shard_map/all_gather | solution.py:100
  70.8 2.1 convolution_convert_fusion.2
  74.4 54.8 %all-gather.7.cloned.1.call-done = bf16[1024,1024]{1,0:T(8,128)(2,1)} async-done(((bf16[32,1024]{1,0:T(8,128)(2,1)}), bf16[1024,1024]{1,0:T(8,128)(2,1)}) %all-gather.7.cloned.1.call-update) | async-done | bytes 2097168 | tf_op jit(solution)/shard_map/all_gather | solution.py:99
  133.4 4.4 all-to-all-start.2
  140.4 3.7 all-to-all-done.2
  145.7 8.7 all-reduce
  154.4 33.1 %all-gather.11.cloned.1.call-done = bf16[1024,1024]{1,0:T(8,128)(2,1)} async-done(((bf16[32,1024]{1,0:T(8,128)(2,1)}), bf16[1024,1024]{1,0:T(8,128)(2,1)}) %all-gather.11.cloned.1.call-update) | async-done | bytes 2097168 | tf_op jit(solution)/shard_map/all_gather | solution.py:98
  187.6 2.1 convolution_convert_fusion.3
  190.6 58.3 %all-gather.15.cloned.1.call-done = bf16[1536,1024]{1,0:T(8,128)(2,1)} async-done(((bf16[192,1024]{1,0:T(8,128)(2,1)}), bf16[1536,1024]{1,0:T(8,128)(2,1)}) %all-gather.15.cloned.1.call-update) | async-done | bytes 3145744 | tf_op jit(solution)/shard_map/all_gather | solution.py:129
  249.0 61.1 %all-gather.9.cloned.1.call-done = bf16[1536,1024]{1,0:T(8,128)(2,1)} async-done(((bf16[192,1024]{1,0:T(8,128)(2,1)}), bf16[1536,1024]{1,0:T(8,128)(2,1)}) %all-gather.9.cloned.1.call-update) | async-done | bytes 3145744 | tf_op jit(solution)/shard_map/all_gather | solution.py:128
  310.1 605.3 %while.15 = (s32[]{:T(128)}, f32[64,16,64]{0,2,1:T(8,128)}, f32[16,64]{1,0:T(8,128)S(1)}, f32[16,64]{1,0:T(8,128)S(1)}, s32[64]{0:T(128)S(1)}, /*index=5*/s32[4,...) while((s32[]{:T(128)}, f32[64,16,64]{0,2,1:T(8,128)}, ...), condition=%wide.region_8.9_spmd.clone, body=%wide.region_5.8_spmd.clone.sunk | while | flops 183465984 | bytes 27471288 | solution.py:155
  310.3 135.5 %gather_fusion = s32[24576]{0:T(1024)S(1)} fusion(s32[1536]{0:T(1024)S(1)} %get-tuple-element.335, s32[24576]{0:T(1024)S(1)} %broadcast_clamp_fusion.2), kind=kCustom, calls=%fused_computation.clone.clone.1 | custom fusion | bytes 294912 | tf_op jit(solution)/shard_map/while/body/eval_jaxpr/jit(_take)/gather | solution.py:31
  450.1 2.4 constant_dynamic-slice_fusion.3
  453.7 4.1 select_reduce_fusion.5
  460.8 135.5 %gather_fusion = s32[24576]{0:T(1024)S(1)} fusion(s32[1536]{0:T(1024)S(1)} %get-tuple-element.335, s32[24576]{0:T(1024)S(1)} %broadcast_clamp_fusion.2), kind=kCustom, calls=%fused_computation.clone.clone.1 | custom fusion | bytes 294912 | tf_op jit(solution)/shard_map/while/body/eval_jaxpr/jit(_take)/gather | solution.py:31
  600.7 2.4 constant_dynamic-slice_fusion.3
  604.2 4.1 select_reduce_fusion.5
  609.8 2.4 fusion.74
  612.4 135.5 %gather_fusion = s32[24576]{0:T(1024)S(1)} fusion(s32[1536]{0:T(1024)S(1)} %get-tuple-element.335, s32[24576]{0:T(1024)S(1)} %broadcast_clamp_fusion.2), kind=kCustom, calls=%fused_computation.clone.clone.1 | custom fusion | bytes 294912 | tf_op jit(solution)/shard_map/while/body/eval_jaxpr/jit(_take)/gather | solution.py:31
  752.3 2.4 constant_dynamic-slice_fusion.3
  755.8 4.1 select_reduce_fusion.5
  761.4 2.4 fusion.74
  764.0 135.5 %gather_fusion = s32[24576]{0:T(1024)S(1)} fusion(s32[1536]{0:T(1024)S(1)} %get-tuple-element.335, s32[24576]{0:T(1024)S(1)} %broadcast_clamp_fusion.2), kind=kCustom, calls=%fused_computation.clone.clone.1 | custom fusion | bytes 294912 | tf_op jit(solution)/shard_map/while/body/eval_jaxpr/jit(_take)/gather | solution.py:31
  903.9 2.4 constant_dynamic-slice_fusion.3
  907.4 4.1 select_reduce_fusion.5
  913.0 2.4 fusion.74
  916.6 2.2 fusion.25
  918.8 10.4 %all_to_all.25 = bf16[8,8,1024]{2,1,0:T(8,128)(2,1)S(1)} all-to-all(bf16[8,8,1024]{2,1,0:T(8,128)(2,1)S(1)} %fusion.25), channel_id=1, replica_groups=mesh['fsdp'=4,'tok'=8] {'tok'}, dimensions={0} | all-to-all | bytes 262144 | tf_op jit(solution)/shard_map/all_to_all | solution.py:168
  (144 shorter events, 48.4 us)
Async XLA Ops:
  7.2 11.9 %copy-start = (bf16[1,64,1024]{2,1,0:T(8,128)(2,1)S(1)}, bf16[1,64,1024]{2,1,0:T(8,128)(2,1)}, u32[]{:S(2)}) copy-start(bf16[1,64,1024]{2,1,0:T(8,128)(2,1)} %param.14) | copy-start | bytes 393220
  7.2 63.6 %all-gather.13.cloned.1.call-start = ((), (), s32[]{:S(2)}) async-start(), calls=%async_computation.7 | async-start | bytes 2162688 | tf_op jit(solution)/shard_map/all_gather | solution.py:100
  7.9 121.3 %all-gather.7.cloned.1.call-start = ((), (), s32[]{:S(2)}) async-start(), calls=%async_computation.4 | async-start | bytes 2162688 | tf_op jit(solution)/shard_map/all_gather | solution.py:99
  8.7 178.9 %all-gather.11.cloned.1.call-start = ((), (), s32[]{:S(2)}) async-start(), calls=%async_computation.6 | async-start | bytes 2162688 | tf_op jit(solution)/shard_map/all_gather | solution.py:98
  10.3 15.1 %copy-start.11 = (s32[64]{0:T(128)}, s32[64]{0:T(128)S(1)}, u32[]{:S(2)}) copy-start(s32[64]{0:T(128)S(1)} %convert_reduce_fusion) | copy-start | bytes 772
  11.8 13.7 %all-to-all-start = ((s32[8,1,8]{2,1,0:T(1,128)}), s32[8,1,8]{2,1,0:T(1,128)S(1)}, u32[]{:S(2)}, u32[]{:S(2)}) async-start(s32[8,1,8]{2,1,0:T(1,128)} %bitcast.1), calls=%async_computation | async-start | bytes 8192 | tf_op jit(solution)/shard_map/all_to_all | solution.py:90
  25.4 10.8 %all-to-all-start.1 = ((bf16[8,8,1024]{2,1,0:T(8,128)(2,1)}), bf16[8,8,1024]{2,1,0:T(8,128)(2,1)S(1)}, u32[]{:S(2)}, u32[]{:S(2)}) async-start(bf16[8,8,1024]{2,1,0:T(8,128)(2,1)} %fusion.26), calls=%async_computation.1 | async-start | bytes 262144 | tf_op jit(solution)/shard_map/all_to_all | solution.py:89
  28.8 220.1 %all-gather.15.cloned.1.call-start = ((), (), s32[]{:S(2)}) async-start(), calls=%async_computation.8 | async-start | bytes 3538944 | tf_op jit(solution)/shard_map/all_gather | solution.py:129
  29.0 116.4 %copy-start.9 = (s32[64]{0:T(128)}, s32[64]{0:T(128)S(1)}, u32[]{:S(2)}) copy-start(s32[64]{0:T(128)S(1)} %sub.69) | copy-start | bytes 772
  29.0 44.5 %copy-start.6 = (bf16[1,128,1024]{2,1,0:T(8,128)(2,1)S(1)}, bf16[1,128,1024]{2,1,0:T(8,128)(2,1)}, u32[]{:S(2)}) copy-start(bf16[1,128,1024]{2,1,0:T(8,128)(2,1)} %param.16) | copy-start | bytes 786436
  36.5 0.7 copy-start.3
  72.9 0.7 copy-start.4
  74.3 57.6 %copy-start.7 = (bf16[1,128,1024]{2,1,0:T(8,128)(2,1)S(1)}, bf16[1,128,1024]{2,1,0:T(8,128)(2,1)}, u32[]{:S(2)}) copy-start(bf16[1,128,1024]{2,1,0:T(8,128)(2,1)} %param.15) | copy-start | bytes 786436
  74.3 64.7 %copy-start.8 = (f32[32,16]{0,1:T(8,128)S(1)}, f32[32,16]{0,1:T(8,128)}, u32[]{:S(2)}) copy-start(f32[32,16]{0,1:T(8,128)} %param.20) | copy-start | bytes 6148
  74.3 64.7 %copy-start.13 = (u32[32]{0:T(128)S(1)}, u32[32]{0:T(128)}, u32[]{:S(2)}) copy-start(u32[32]{0:T(128)} %constant.64) | copy-start | bytes 388
  74.4 235.7 %all-gather.9.cloned.1.call-start = ((), (), s32[]{:S(2)}) async-start(), calls=%async_computation.5 | async-start | bytes 3538944 | tf_op jit(solution)/shard_map/all_gather | solution.py:128
  131.3 0.7 copy-start.5
  133.4 10.8 %all-to-all-start.2 = ((s32[8,1,8]{2,1,0:T(1,128)}), s32[8,1,8]{2,1,0:T(1,128)S(1)}, u32[]{:S(2)}, u32[]{:S(2)}) async-start(s32[8,1,8]{2,1,0:T(1,128)} %bitcast.6), calls=%async_computation.2 | async-start | bytes 8192 | tf_op jit(solution)/shard_map/all_to_all | solution.py:91
  137.8 778.8 %all-gather.17.cloned.1.call-start = ((), (), s32[]{:S(2)}) async-start(), calls=%async_computation.9 | async-start | bytes 2162688 | tf_op jit(solution)/shard_map/all_gather | solution.py:101
  154.4 155.7 %copy-start.1 = (s32[1536]{0:T(1024)S(1)}, s32[1536]{0:T(1024)}, u32[]{:S(2)}) copy-start(s32[1536]{0:T(1024)} %param.19) | copy-start | bytes 18436
  310.1 606.5 %copy-start.10 = (s32[64]{0:T(128)S(1)}, s32[64]{0:T(128)}, u32[]{:S(2)}) copy-start(s32[64]{0:T(128)} %copy-done.9) | copy-start | bytes 772
  457.8 1.2 copy-start.2
  608.3 1.2 copy-start.2
  759.9 1.2 copy-start.2
  911.5 1.2 copy-start.2
  916.5 12.7 %copy-start.12 = (s32[64]{0:T(128)S(1)}, s32[64]{0:T(128)}, u32[]{:S(2)}) copy-start(s32[64]{0:T(128)} %copy-done.11) | copy-start | bytes 772
Sparse Core Ops, SparseCore 0:
  11.0 59.7 all-gather.12
  73.8 55.3 all-gather.6
  132.2 55.3 all-gather.10
  189.6 59.2 all-gather.14
  251.0 59.0 all-gather.8
  312.9 55.1 all-gather.16
where the time goes:
time: 938 us; the launch traced here: 937 us
  local copies, waits for them, and re-layouts  566 us (60%)
  waiting for transfers between devices  259 us (28%)
  matrix products  51.5 us (5%)
  blocking collectives  19.1 us (2%)
  between operations  15.7 us (2%)
  starting transfers between devices  15.3 us (2%)
  other arithmetic  9.68 us (1%)
    gather x8, local copies, waits for them, and re-layouts, absorb(): jnp.take(bucket_table, jnp.clip(distance, 0, bucket_table.shape[0] - 1),...  542 us
    all_gather x1, waiting for transfers between devices, shards(): part_keys = lax.all_gather(keys_here, 'tok', axis=0, tiled=True)  61.1 us
    all_gather x1, waiting for transfers between devices, shards(): part_values = lax.all_gather(values_here, 'tok', axis=0, tiled=True)  58.3 us
    all_gather x1, waiting for transfers between devices, shards(): lax.all_gather(w_key, ('fsdp', 'tok'), axis=0, tiled=True)  54.8 us
    all_gather x1, waiting for transfers between devices, shards(): lax.all_gather(w_query, ('fsdp', 'tok'), axis=0, tiled=True)  33.1 us
    all_gather x1, waiting for transfers between devices, shards(): lax.all_gather(w_value, ('fsdp', 'tok'), axis=0, tiled=True)  32.8 us
  transfers between devices with their start and end apart: 9, of which 8 were waited for; matrix products, arithmetic and copies ran while one was open for 66% of the time, Pallas kernels for 0%

commit v1 on v0

--- a/solution.py
+++ b/solution.py
@@ -5,6 +5,28 @@
 
 far_away = 1073741824
 neg_floor = -1e30
+
+
+def finish_views_up(x_local, dim_k):
+    x_local = jnp.moveaxis(x_local, 0, dim_k)
+    answer = x_local.shape
+    return x_local.reshape(*answer[:dim_k], answer[dim_k] * answer[dim_k + 1], *answer[dim_k + 2 :])
+
+
+def state_track(xs, which_axis):
+    val2 = lax.axis_size(which_axis)
+    piece_out = lax.axis_index(which_axis)
+    mat_out, known = (val2, piece_out)
+    response, piece_next = (xs[None], 1)
+    while piece_next < mat_out:
+        heard = tuple(((tick, tick ^ piece_next) for tick in range(mat_out)))
+        state_now = lax.ppermute(response, which_axis, heard)
+        row_out = known & piece_next == 0
+        odd = jnp.where(row_out, response, state_now)
+        shaped = jnp.where(row_out, state_now, response)
+        response = jnp.concatenate([odd, shaped])
+        piece_next *= 2
+    return response
 
 
 def bias_scores(bucket_ids, bias_parts):
@@ -94,8 +116,13 @@
     place_sel = local_slot[None, :] == row_iota[:, None]
     dealt = permute_rows(place_sel, got_rows.reshape(tok_rows, feature_count))
     dealt_pos = permute_ints(place_sel, got_pos.reshape(tok_rows))
+
+    def entries_get(payload, frame, where_dim):
+        reply = state_track(payload, frame)
+        return finish_views_up(reply, where_dim)
+
     query_w, key_w, value_w, out_w = (
-        lax.all_gather(w_query, ("fsdp", "tok"), axis=0, tiled=True),
+        entries_get(w_query, ("fsdp", "tok"), 0),
         lax.all_gather(w_key, ("fsdp", "tok"), axis=0, tiled=True),
         lax.all_gather(w_value, ("fsdp", "tok"), axis=0, tiled=True),
         lax.all_gather(w_out, ("fsdp", "tok"), axis=0, tiled=True),

time: 938 us -> 890 us (0.949)
  waiting for transfers between devices: 259 us -> 209 us
    all_gather x1, waiting for transfers between devices: 58.3 us -> 5.13 us  [shards(): part_values = lax.all_gather(values_here, 'tok', axis=0, tiled=True)]
    ppermute x0 -> x5, waiting for transfers between devices: none -> 35.6 us  [state_track(): state_now = lax.ppermute(response, which_axis, heard)]
    all_gather x1 -> x0, waiting for transfers between devices: 33.1 us -> none  [shards(): lax.all_gather(w_query, ('fsdp', 'tok'), axis=0, tiled=True)]
  transfers between devices with their start and end apart: 9 -> 13, of which waited for: 8 -> 12; matrix products, arithmetic and copies ran while one was open for 66% -> 70% of each run, Pallas kernels for 0% -> 0%
where the time goes in v1:
time: 890 us; the launch traced here: 889 us
  local copies, waits for them, and re-layouts  566 us (64%)
  waiting for transfers between devices  209 us (23%)
  matrix products  50.1 us (6%)
  blocking collectives  19.2 us (2%)
  starting transfers between devices  18.3 us (2%)
  between operations  15.4 us (2%)
  other arithmetic  11.4 us (1%)
    gather x8, local copies, waits for them, and re-layouts, absorb(): jnp.take(bucket_table, jnp.clip(distance, 0, bucket_table.shape[0] - 1),...  542 us
    all_gather x1, waiting for transfers between devices, shards(): part_keys = lax.all_gather(keys_here, 'tok', axis=0, tiled=True)  61.1 us
    all_gather x1, waiting for transfers between devices, shards(): lax.all_gather(w_key, ('fsdp', 'tok'), axis=0, tiled=True)  54.8 us
    ppermute x5, waiting for transfers between devices, state_track(): state_now = lax.ppermute(response, which_axis, heard)  35.6 us
    all_gather x1, waiting for transfers between devices, shards(): lax.all_gather(w_value, ('fsdp', 'tok'), axis=0, tiled=True)  33.2 us
  transfers between devices with their start and end apart: 13, of which 12 were waited for; matrix products, arithmetic and copies ran while one was open for 70% of the time, Pallas kernels for 0%

profile of v1, /device:TPU:0, one launch (start us, length us, event | category | flops | bytes accessed | tf_op | source)
XLA Modules:
  0.0 889.4 jit_solution(1824857813488719651)
XLA Ops:
  11.0 7.3 all-to-all-start
  19.2 5.6 all-to-all-done
  24.7 3.4 all-to-all-start.1
  28.3 7.3 all-to-all-done.1
  37.3 33.2 %all-gather.10.cloned.1.call-done = bf16[1024,1024]{1,0:T(8,128)(2,1)} async-done(((bf16[32,1024]{1,0:T(8,128)(2,1)}), bf16[1024,1024]{1,0:T(8,128)(2,1)}) %all-gather.10.cloned.1.call-update) | async-done | bytes 2097168 | tf_op jit(solution)/shard_map/all_gather | solution.py:127
  74.1 54.8 %all-gather.6.cloned.1.call-done = bf16[1024,1024]{1,0:T(8,128)(2,1)} async-done(((bf16[32,1024]{1,0:T(8,128)(2,1)}), bf16[1024,1024]{1,0:T(8,128)(2,1)}) %all-gather.6.cloned.1.call-update) | async-done | bytes 2097168 | tf_op jit(solution)/shard_map/all_gather | solution.py:126
  134.0 2.8 collective-permute-done
  137.5 7.9 collective-permute-done.1
  145.5 20.3 %collective-permute-done.2 = bf16[4,32,1024]{2,1,0:T(8,128)(2,1)S(1)} collective-permute-done((bf16[4,32,1024]{2,1,0:T(8,128)(2,1)S(1)}, bf16[4,32,1024]{2,1,0:T(8,128)(2,1)S(1)}, u32[]{:S(2)}, u32[]{:S(2)}) %collective-permute-start.2) | collective-permute-done | bytes 262176 | tf_op jit(solution)/shard_map/ppermute | solution.py:23
  171.3 3.6 all-to-all-start.2
  177.5 3.9 all-to-all-done.2
  183.0 8.8 all-reduce
  191.8 2.7 collective-permute-done.4
  196.4 5.1 all-gather.12.cloned.1.call-done
  201.5 61.1 %all-gather.8.cloned.1.call-done = bf16[1536,1024]{1,0:T(8,128)(2,1)} async-done(((bf16[192,1024]{1,0:T(8,128)(2,1)}), bf16[1536,1024]{1,0:T(8,128)(2,1)}) %all-gather.8.cloned.1.call-update) | async-done | bytes 3145744 | tf_op jit(solution)/shard_map/all_gather | solution.py:155
  262.7 605.5 %while.15 = (s32[]{:T(128)}, f32[64,16,64]{0,2,1:T(8,128)}, f32[16,64]{1,0:T(8,128)S(1)}, f32[16,64]{1,0:T(8,128)S(1)}, s32[64]{0:T(128)S(1)}, /*index=5*/s32[4,...) while((s32[]{:T(128)}, f32[64,16,64]{0,2,1:T(8,128)}, ...), condition=%wide.region_8.9_spmd.clone, body=%wide.region_5.8_spmd.clone.sunk | while | flops 183465984 | bytes 27471288 | solution.py:182
  262.8 135.5 %gather_fusion = s32[24576]{0:T(1024)S(1)} fusion(s32[1536]{0:T(1024)S(1)} %get-tuple-element.345, s32[24576]{0:T(1024)S(1)} %broadcast_clamp_fusion.2), kind=kCustom, calls=%fused_computation.clone.clone.1 | custom fusion | bytes 294912 | tf_op jit(solution)/shard_map/while/body/eval_jaxpr/jit(_take)/gather | solution.py:53
  402.7 2.4 constant_dynamic-slice_fusion.3
  406.3 4.1 select_reduce_fusion.5
  413.4 135.5 %gather_fusion = s32[24576]{0:T(1024)S(1)} fusion(s32[1536]{0:T(1024)S(1)} %get-tuple-element.345, s32[24576]{0:T(1024)S(1)} %broadcast_clamp_fusion.2), kind=kCustom, calls=%fused_computation.clone.clone.1 | custom fusion | bytes 294912 | tf_op jit(solution)/shard_map/while/body/eval_jaxpr/jit(_take)/gather | solution.py:53
  553.3 2.4 constant_dynamic-slice_fusion.3
  556.9 4.1 select_reduce_fusion.5
  562.5 2.4 fusion.74
  565.1 135.5 %gather_fusion = s32[24576]{0:T(1024)S(1)} fusion(s32[1536]{0:T(1024)S(1)} %get-tuple-element.345, s32[24576]{0:T(1024)S(1)} %broadcast_clamp_fusion.2), kind=kCustom, calls=%fused_computation.clone.clone.1 | custom fusion | bytes 294912 | tf_op jit(solution)/shard_map/while/body/eval_jaxpr/jit(_take)/gather | solution.py:53
  705.0 2.4 constant_dynamic-slice_fusion.3
  708.6 4.1 select_reduce_fusion.5
  714.2 2.4 fusion.74
  716.7 135.5 %gather_fusion = s32[24576]{0:T(1024)S(1)} fusion(s32[1536]{0:T(1024)S(1)} %get-tuple-element.345, s32[24576]{0:T(1024)S(1)} %broadcast_clamp_fusion.2), kind=kCustom, calls=%fused_computation.clone.clone.1 | custom fusion | bytes 294912 | tf_op jit(solution)/shard_map/while/body/eval_jaxpr/jit(_take)/gather | solution.py:53
  856.6 2.4 constant_dynamic-slice_fusion.3
  860.2 4.1 select_reduce_fusion.5
  865.8 2.4 fusion.74
  871.6 10.4 %all_to_all.25 = bf16[8,8,1024]{2,1,0:T(8,128)(2,1)S(1)} all-to-all(bf16[8,8,1024]{2,1,0:T(8,128)(2,1)S(1)} %fusion.25), channel_id=1, replica_groups=mesh['fsdp'=4,'tok'=8] {'tok'}, dimensions={0} | all-to-all | bytes 262144 | tf_op jit(solution)/shard_map/all_to_all | solution.py:195
  (163 shorter events, 60.1 us)
Async XLA Ops:
  7.2 11.2 %copy-start = (bf16[1,64,1024]{2,1,0:T(8,128)(2,1)S(1)}, bf16[1,64,1024]{2,1,0:T(8,128)(2,1)}, u32[]{:S(2)}) copy-start(bf16[1,64,1024]{2,1,0:T(8,128)(2,1)} %param.14) | copy-start | bytes 393220
  7.2 63.3 %all-gather.10.cloned.1.call-start = ((), (), s32[]{:S(2)}) async-start(), calls=%async_computation.6 | async-start | bytes 2162688 | tf_op jit(solution)/shard_map/all_gather | solution.py:127
  7.9 121.0 %all-gather.6.cloned.1.call-start = ((), (), s32[]{:S(2)}) async-start(), calls=%async_computation.4 | async-start | bytes 2162688 | tf_op jit(solution)/shard_map/all_gather | solution.py:126
  9.6 15.1 %copy-start.12 = (s32[64]{0:T(128)}, s32[64]{0:T(128)S(1)}, u32[]{:S(2)}) copy-start(s32[64]{0:T(128)S(1)} %convert_reduce_fusion) | copy-start | bytes 772
  11.0 13.7 %all-to-all-start = ((s32[8,1,8]{2,1,0:T(1,128)}), s32[8,1,8]{2,1,0:T(1,128)S(1)}, u32[]{:S(2)}, u32[]{:S(2)}) async-start(s32[8,1,8]{2,1,0:T(1,128)} %bitcast.1), calls=%async_computation | async-start | bytes 8192 | tf_op jit(solution)/shard_map/all_to_all | solution.py:112
  24.7 10.8 %all-to-all-start.1 = ((bf16[8,8,1024]{2,1,0:T(8,128)(2,1)}), bf16[8,8,1024]{2,1,0:T(8,128)(2,1)S(1)}, u32[]{:S(2)}, u32[]{:S(2)}) async-start(bf16[8,8,1024]{2,1,0:T(8,128)(2,1)} %fusion.26), calls=%async_computation.1 | async-start | bytes 262144 | tf_op jit(solution)/shard_map/all_to_all | solution.py:111
  28.1 173.4 %all-gather.12.cloned.1.call-start = ((), (), s32[]{:S(2)}) async-start(), calls=%async_computation.7 | async-start | bytes 3538944 | tf_op jit(solution)/shard_map/all_gather | solution.py:156
  28.3 154.5 %copy-start.10 = (s32[64]{0:T(128)}, s32[64]{0:T(128)S(1)}, u32[]{:S(2)}) copy-start(s32[64]{0:T(128)S(1)} %sub.69) | copy-start | bytes 772
  28.3 45.0 %copy-start.6 = (bf16[1,128,1024]{2,1,0:T(8,128)(2,1)S(1)}, bf16[1,128,1024]{2,1,0:T(8,128)(2,1)}, u32[]{:S(2)}) copy-start(bf16[1,128,1024]{2,1,0:T(8,128)(2,1)} %param.16) | copy-start | bytes 786436
  35.8 0.7 copy-start.3
  72.6 0.7 copy-start.4
  74.1 57.6 %copy-start.7 = (bf16[1,128,1024]{2,1,0:T(8,128)(2,1)S(1)}, bf16[1,128,1024]{2,1,0:T(8,128)(2,1)}, u32[]{:S(2)}) copy-start(bf16[1,128,1024]{2,1,0:T(8,128)(2,1)} %param.15) | copy-start | bytes 786436
  74.1 58.4 %copy-start.8 = (bf16[32,1024]{1,0:T(8,128)(2,1)S(1)}, bf16[32,1024]{1,0:T(8,128)(2,1)}, u32[]{:S(2)}) copy-start(bf16[32,1024]{1,0:T(8,128)(2,1)} %param.22) | copy-start | bytes 196612
  74.1 188.6 %all-gather.8.cloned.1.call-start = ((), (), s32[]{:S(2)}) async-start(), calls=%async_computation.5 | async-start | bytes 3538944 | tf_op jit(solution)/shard_map/all_gather | solution.py:155
  131.0 0.7 copy-start.5
  132.4 4.3 collective-permute-start
  136.8 8.5 collective-permute-start.1
  145.4 20.4 %collective-permute-start.2 = (bf16[4,32,1024]{2,1,0:T(8,128)(2,1)S(1)}, bf16[4,32,1024]{2,1,0:T(8,128)(2,1)S(1)}, u32[]{:S(2)}, u32[]{:S(2)}) collective-permute-start(bf16[4,32,1024]{2,1,0:T(8,128)(2,1)S(1)} %pad_maximum_fusion.5), channel_id=1, source_target_pairs={{0,4},{1,5},{2,6},{3,7},{4,0},{5,1},{6,2},{7,3},{8,12},{9,13},{10,... | collective-permute-start | bytes 786440 | tf_op jit(solution)/shard_map/ppermute | solution.py:23
  165.9 2.0 collective-permute-start.3
  168.0 8.2 copy-start.9
  168.0 8.3 copy-start.14
  169.2 25.4 %collective-permute-start.4 = (bf16[16,32,1024]{2,1,0:T(8,128)(2,1)}, bf16[16,32,1024]{2,1,0:T(8,128)(2,1)S(1)}, u32[]{:S(2)}, u32[]{:S(2)}) collective-permute-start(bf16[16,32,1024]{2,1,0:T(8,128)(2,1)} %pad_maximum_fusion.1), channel_id=1, source_target_pairs={{0,16},{1,17},{2,18},{3,19},{4,20},{5,21},{6,22},{7,23},{8,24},{9,... | collective-permute-start | bytes 3145736 | tf_op jit(solution)/shard_map/ppermute | solution.py:23
  171.3 10.2 %all-to-all-start.2 = ((s32[8,1,8]{2,1,0:T(1,128)}), s32[8,1,8]{2,1,0:T(1,128)S(1)}, u32[]{:S(2)}, u32[]{:S(2)}) async-start(s32[8,1,8]{2,1,0:T(1,128)} %bitcast.6), calls=%async_computation.2 | async-start | bytes 8192 | tf_op jit(solution)/shard_map/all_to_all | solution.py:113
  174.9 694.4 %all-gather.14.cloned.1.call-start = ((), (), s32[]{:S(2)}) async-start(), calls=%async_computation.8 | async-start | bytes 2162688 | tf_op jit(solution)/shard_map/all_gather | solution.py:128
  194.9 67.7 %copy-start.1 = (s32[1536]{0:T(1024)S(1)}, s32[1536]{0:T(1024)}, u32[]{:S(2)}) copy-start(s32[1536]{0:T(1024)} %param.19) | copy-start | bytes 18436
  262.7 606.7 %copy-start.11 = (s32[64]{0:T(128)S(1)}, s32[64]{0:T(128)}, u32[]{:S(2)}) copy-start(s32[64]{0:T(128)} %copy-done.10) | copy-start | bytes 772
  410.4 1.2 copy-start.2
  561.0 1.2 copy-start.2
  712.6 1.2 copy-start.2
  864.3 1.2 copy-start.2
  869.3 12.7 %copy-start.13 = (s32[64]{0:T(128)S(1)}, s32[64]{0:T(128)}, u32[]{:S(2)}) copy-start(s32[64]{0:T(128)} %copy-done.12) | copy-start | bytes 772
Sparse Core Ops, SparseCore 0:
  11.0 59.4 all-gather.9
  73.5 55.3 all-gather.5
  131.1 70.3 all-gather.11
  203.6 59.0 all-gather.7
  265.5 55.1 all-gather.13
